TPU v7x, 128 devices: a whole 4x4x4 slice. The times are simulated.
128 devices in a mesh: row: 8 (over z, y_hi), col: 4 (over y_lo, core), feat: 4 (over x).
Axes of the slice: x: 4, y: 4 (y_hi: 2, y_lo: 2; y = y_hi * 2 + y_lo), z: 4, core: 2. Of those that a mesh axis runs over, the one named last changes fastest.
Arguments:
- features: bfloat16 [262144, 128], P(('row', 'col'), 'feat'), may hold values from -6 to 6
- tiles: bfloat16 [8, 4, 1536, 128, 128], P('row', 'col', 'feat'), may hold values from 0 to 0.04321289
- tile_row: int32 [8, 4, 1536], P('row', 'col', 'feat'), may hold values from 0 to 255
- tile_col: int32 [8, 4, 1536], P('row', 'col', 'feat'), may hold values from 0 to 511
- tile_count: int32 [8, 4, 4], P('row', 'col', 'feat'), may hold values from 1 to 384, as said below
- weight: bfloat16 [128, 256], replicated, may hold values from -0.5 to 0.5
- bias: float32 [256], replicated, may hold values from -3 to 3
Outputs:
- output: bfloat16 [262144, 256], P(('row', 'col', 'feat'))
Inputs may be any that keep to these rules, and one draw needn't show every extreme that they name: `tile_count`: some device has all 384 slots live.
All inputs are finite; a program needn't handle non-finite values.
Results may differ from a plain program's by a relative error of at most 0.02.
Values may be sent and summed in bfloat16 or wider, within the bound.
No kernel may reach another device: no remote copies, remote signals or barrier semaphores. Data moves between devices by JAX's collectives and lax.ppermute only.
A program may use at most 128 MiB of HBM per device.

v0:
```python
import jax
import jax.numpy as jnp
from jax import lax
from jax.sharding import PartitionSpec as P


def body(features, tiles, tile_row, tile_col, tile_count, weight, bias):
    node_rows = lax.all_to_all(features, "feat", split_axis=0, concat_axis=1, tiled=True)
    sources = lax.all_gather(node_rows, ("row", "feat"), axis=0, tiled=True)
    tile_side = tiles.shape[-1]
    width = sources.shape[1]
    node_dev = features.shape[0] // lax.axis_size("feat")
    block_rows = lax.axis_size("col") * lax.axis_size("feat") * node_dev // tile_side
    src_blocks = sources.reshape(-1, tile_side, width)
    slot_total = tiles.shape[2]
    tile_stack = tiles.reshape(slot_total, tile_side, tile_side)
    row_index = tile_row.reshape(slot_total)
    col_index = tile_col.reshape(slot_total)
    live_count = tile_count.reshape(())
    block = min(32, slot_total)
    turns = (live_count + block - 1) // block

    def one_turn(turn, partial_value):
        start = turn * block
        tile_block = lax.dynamic_slice_in_dim(tile_stack, start, block, 0)
        rows_here = lax.dynamic_slice_in_dim(row_index, start, block, 0)
        cols_here = lax.dynamic_slice_in_dim(col_index, start, block, 0)
        picked = jnp.take(src_blocks, cols_here, axis=0)
        prods = jnp.einsum("tij,tjf->tif", tile_block, picked, preferred_element_type=jnp.float32)
        live = start + jnp.arange(block, dtype=jnp.int32) < live_count
        prods = jnp.where(live[:, None, None], prods, jnp.zeros_like(prods))
        return partial_value.at[rows_here].add(prods)

    empty = jnp.zeros((block_rows, tile_side, width), jnp.float32)
    partial_value = lax.fori_loop(0, turns, one_turn, empty)
    rounded = lax.optimization_barrier(
        partial_value.reshape(block_rows * tile_side, width).astype(jnp.bfloat16)
    )
    terms = rounded.astype(jnp.float32)
    agg = lax.psum_scatter(
        terms.astype(jnp.bfloat16), ("col", "feat"), scatter_dimension=0, tiled=True
    )
    hidden = jnp.dot(agg, weight, preferred_element_type=jnp.float32) + bias
    return jax.nn.relu(hidden).astype(jnp.bfloat16)


def solution(mesh):
    placed = (
        P(("row", "col"), "feat"),
        P("row", "col", "feat", None, None),
        P("row", "col", "feat"),
        P("row", "col", "feat"),
        P("row", "col", "feat"),
        P(),
        P(),
    )
    return jax.shard_map(
        body, mesh=mesh, in_specs=placed, out_specs=P(("row", "col", "feat"), None), check_vma=False
    )
```

profile of v0, /device:TPU:1, one launch (start us, length us, event | category | flops | bytes accessed | tf_op | source)
XLA Modules:
  0.0 501.4 jit_solution(782019901176667349)
XLA Ops:
  6.5 0.0 copy-start
  6.5 0.0 all-gather.2.cloned.1.call-start
  6.5 1.1 copy.17
  7.7 13.3 %all_to_all.19 = bf16[4,2048,32]{1,2,0:T(8,128)(2,1)} all-to-all(bf16[4,2048,32]{1,2,0:T(8,128)(2,1)S(1)} %bitcast.18), channel_id=1, replica_groups=mesh['row'=8,'col'=4,'feat'=4] {'feat'}, dimensions={0} | all-to-all | bytes 1048576 | tf_op jit(solution)/shard_map/all_to_all | solution.py:8
  21.0 0.0 all-gather.2.cloned.1.call-update
  21.0 0.0 reduce-scatter.2.cloned.1.call-start
  21.7 0.7 reduce
  22.4 0.7 reduce.1
  23.1 150.9 %all-gather.2.cloned.1.call-done = bf16[65536,128]{0,1:T(8,128)(2,1)} async-done(((bf16[2048,128]{0,1:T(8,128)(2,1)}), bf16[65536,128]{0,1:T(8,128)(2,1)}) %all-gather.2.cloned.1.call-update) | async-done | bytes 16777232 | tf_op jit(solution)/shard_map/all_gather | solution.py:9
  174.0 22.4 %copy.14 = bf16[65536,128]{1,0:T(8,128)(2,1)} copy(bf16[65536,128]{0,1:T(8,128)(2,1)} %all-gather.2.cloned.1.call-done) | data formatting | bytes 33554432 | tf_op jit(solution)/shard_map/while | solution.py:35
  196.4 7.8 %broadcast_in_dim.28 = f32[256,128,128]{2,1,0:T(8,128)} broadcast(f32[]{:T(128)} %constant.47.clone.1), dimensions={} | broadcast | bytes 16777220 | tf_op jit(solution)/shard_map/broadcast_in_dim | solution.py:34
  204.3 106.8 %while.10 = (s32[]{:T(128)}, f32[256,128,128]{2,1,0:T(8,128)}, s32[]{:T(128)}, s32[384]{0:T(512)S(1)}, s32[]{:T(128)}, /*index=5*/bf16[384,128,128]{2,1,0:T(8,12...) while((s32[]{:T(128)}, f32[256,128,128]{2,1,0:T(8,128)}, ...), condition=%wide.region_2.3_spmd, body=%wide.region_0.2_spmd.sunk | while | flops 135791968 | bytes 12588215 | solution.py:35
  204.3 0.1 compare_select_fusion.4
  204.4 0.7 compare_and_fusion.2
  205.1 6.5 %gather_fusion = bf16[32,128,128]{2,1,0:T(8,128)(2,1)S(1)} fusion(bf16[512,128,128]{2,1,0:T(8,128)(2,1)} %get-tuple-element.179, s32[1024]{0:T(1024)S(1)} %pad_clamp_fusion.2), kind=kCustom, calls=%fused_computation.clone.1 | custom fusion | bytes 2097280 | tf_op jit(solution)/shard_map/while/body/jit(_take)/gather | solution.py:28
  211.6 1.7 convolution_select_fusion.2
  213.4 6.2 %scatter_fusion = f32[256,128,128]{2,1,0:T(8,128)} fusion(f32[256,128,128]{2,1,0:T(8,128)} %get-tuple-element.161, s32[32]{0:T(128)S(1)} %compare_select_fusion.4, f32[32,128,128]{2,1,0:T(8,128)S(1)} %convolution_select_fusion.2), kind=kCustom, calls=%fused_computation.1.clone.1 | custom fusion | flops 524288 | bytes 6291584 | tf_op jit(solution)/shard_map/while/body/scatter-add | solution.py:32
  219.6 0.1 compare_select_fusion.4
  219.7 0.7 compare_and_fusion.2
  220.4 6.5 %gather_fusion = bf16[32,128,128]{2,1,0:T(8,128)(2,1)S(1)} fusion(bf16[512,128,128]{2,1,0:T(8,128)(2,1)} %get-tuple-element.179, s32[1024]{0:T(1024)S(1)} %pad_clamp_fusion.2), kind=kCustom, calls=%fused_computation.clone.1 | custom fusion | bytes 2097280 | tf_op jit(solution)/shard_map/while/body/jit(_take)/gather | solution.py:28
  226.9 1.7 convolution_select_fusion.2
  228.7 6.2 %scatter_fusion = f32[256,128,128]{2,1,0:T(8,128)} fusion(f32[256,128,128]{2,1,0:T(8,128)} %get-tuple-element.161, s32[32]{0:T(128)S(1)} %compare_select_fusion.4, f32[32,128,128]{2,1,0:T(8,128)S(1)} %convolution_select_fusion.2), kind=kCustom, calls=%fused_computation.1.clone.1 | custom fusion | flops 524288 | bytes 6291584 | tf_op jit(solution)/shard_map/while/body/scatter-add | solution.py:32
  234.9 0.1 compare_select_fusion.4
  235.0 0.7 compare_and_fusion.2
  235.7 6.5 %gather_fusion = bf16[32,128,128]{2,1,0:T(8,128)(2,1)S(1)} fusion(bf16[512,128,128]{2,1,0:T(8,128)(2,1)} %get-tuple-element.179, s32[1024]{0:T(1024)S(1)} %pad_clamp_fusion.2), kind=kCustom, calls=%fused_computation.clone.1 | custom fusion | bytes 2097280 | tf_op jit(solution)/shard_map/while/body/jit(_take)/gather | solution.py:28
  242.2 1.7 convolution_select_fusion.2
  244.0 6.1 %scatter_fusion = f32[256,128,128]{2,1,0:T(8,128)} fusion(f32[256,128,128]{2,1,0:T(8,128)} %get-tuple-element.161, s32[32]{0:T(128)S(1)} %compare_select_fusion.4, f32[32,128,128]{2,1,0:T(8,128)S(1)} %convolution_select_fusion.2), kind=kCustom, calls=%fused_computation.1.clone.1 | custom fusion | flops 524288 | bytes 6291584 | tf_op jit(solution)/shard_map/while/body/scatter-add | solution.py:32
  250.1 0.1 compare_select_fusion.4
  250.2 0.7 compare_and_fusion.2
  250.9 6.5 %gather_fusion = bf16[32,128,128]{2,1,0:T(8,128)(2,1)S(1)} fusion(bf16[512,128,128]{2,1,0:T(8,128)(2,1)} %get-tuple-element.179, s32[1024]{0:T(1024)S(1)} %pad_clamp_fusion.2), kind=kCustom, calls=%fused_computation.clone.1 | custom fusion | bytes 2097280 | tf_op jit(solution)/shard_map/while/body/jit(_take)/gather | solution.py:28
  257.4 1.7 convolution_select_fusion.2
  259.2 6.2 %scatter_fusion = f32[256,128,128]{2,1,0:T(8,128)} fusion(f32[256,128,128]{2,1,0:T(8,128)} %get-tuple-element.161, s32[32]{0:T(128)S(1)} %compare_select_fusion.4, f32[32,128,128]{2,1,0:T(8,128)S(1)} %convolution_select_fusion.2), kind=kCustom, calls=%fused_computation.1.clone.1 | custom fusion | flops 524288 | bytes 6291584 | tf_op jit(solution)/shard_map/while/body/scatter-add | solution.py:32
  265.4 0.1 compare_select_fusion.4
  265.5 0.7 compare_and_fusion.2
  266.2 6.5 %gather_fusion = bf16[32,128,128]{2,1,0:T(8,128)(2,1)S(1)} fusion(bf16[512,128,128]{2,1,0:T(8,128)(2,1)} %get-tuple-element.179, s32[1024]{0:T(1024)S(1)} %pad_clamp_fusion.2), kind=kCustom, calls=%fused_computation.clone.1 | custom fusion | bytes 2097280 | tf_op jit(solution)/shard_map/while/body/jit(_take)/gather | solution.py:28
  272.8 1.7 convolution_select_fusion.2
  274.5 6.2 %scatter_fusion = f32[256,128,128]{2,1,0:T(8,128)} fusion(f32[256,128,128]{2,1,0:T(8,128)} %get-tuple-element.161, s32[32]{0:T(128)S(1)} %compare_select_fusion.4, f32[32,128,128]{2,1,0:T(8,128)S(1)} %convolution_select_fusion.2), kind=kCustom, calls=%fused_computation.1.clone.1 | custom fusion | flops 524288 | bytes 6291584 | tf_op jit(solution)/shard_map/while/body/scatter-add | solution.py:32
  280.7 0.1 compare_select_fusion.4
  280.8 0.7 compare_and_fusion.2
  281.5 6.5 %gather_fusion = bf16[32,128,128]{2,1,0:T(8,128)(2,1)S(1)} fusion(bf16[512,128,128]{2,1,0:T(8,128)(2,1)} %get-tuple-element.179, s32[1024]{0:T(1024)S(1)} %pad_clamp_fusion.2), kind=kCustom, calls=%fused_computation.clone.1 | custom fusion | bytes 2097280 | tf_op jit(solution)/shard_map/while/body/jit(_take)/gather | solution.py:28
  288.0 1.7 convolution_select_fusion.2
  289.8 6.1 %scatter_fusion = f32[256,128,128]{2,1,0:T(8,128)} fusion(f32[256,128,128]{2,1,0:T(8,128)} %get-tuple-element.161, s32[32]{0:T(128)S(1)} %compare_select_fusion.4, f32[32,128,128]{2,1,0:T(8,128)S(1)} %convolution_select_fusion.2), kind=kCustom, calls=%fused_computation.1.clone.1 | custom fusion | flops 524288 | bytes 6291584 | tf_op jit(solution)/shard_map/while/body/scatter-add | solution.py:32
  295.9 0.1 compare_select_fusion.4
  296.0 0.7 compare_and_fusion.2
  296.7 6.5 %gather_fusion = bf16[32,128,128]{2,1,0:T(8,128)(2,1)S(1)} fusion(bf16[512,128,128]{2,1,0:T(8,128)(2,1)} %get-tuple-element.179, s32[1024]{0:T(1024)S(1)} %pad_clamp_fusion.2), kind=kCustom, calls=%fused_computation.clone.1 | custom fusion | bytes 2097280 | tf_op jit(solution)/shard_map/while/body/jit(_take)/gather | solution.py:28
  303.2 1.7 convolution_select_fusion.2
  305.0 6.1 %scatter_fusion = f32[256,128,128]{2,1,0:T(8,128)} fusion(f32[256,128,128]{2,1,0:T(8,128)} %get-tuple-element.161, s32[32]{0:T(128)S(1)} %compare_select_fusion.4, f32[32,128,128]{2,1,0:T(8,128)S(1)} %convolution_select_fusion.2), kind=kCustom, calls=%fused_computation.1.clone.1 | custom fusion | flops 524288 | bytes 6291584 | tf_op jit(solution)/shard_map/while/body/scatter-add | solution.py:32
  311.1 0.0 copy-start.1
  311.1 9.2 %convert_element_type.11 = bf16[256,128,128]{2,1,0:T(8,128)(2,1)} convert(f32[256,128,128]{2,1,0:T(8,128)} %get-tuple-element.48) | non-fusion elementwise | flops 4194304 | bytes 25165824 | tf_op jit(solution)/shard_map/convert_element_type | solution.py:37
  320.3 0.0 reduce-scatter.2.cloned.1.call-update
  320.3 171.8 %reduce-scatter.2.cloned.1.call-done = bf16[2048,128]{1,0:T(8,128)(2,1)} async-done(((bf16[32768,128]{1,0:T(8,128)(2,1)}), bf16[2048,128]{1,0:T(8,128)(2,1)}) %reduce-scatter.2.cloned.1.call-update) | async-done | bytes 524304 | tf_op jit(solution)/shard_map/reduce_scatter | solution.py:40
  492.2 0.0 copy-done
  492.2 0.0 copy-done.1
  492.2 2.4 fusion.7
  (7 shorter events, 0.0 us)
Async XLA Ops:
  6.5 485.6 %copy-start = (bf16[128,256]{1,0:T(8,128)(2,1)S(1)}, bf16[128,256]{1,0:T(8,128)(2,1)}, u32[]{:S(2)}) copy-start(bf16[128,256]{1,0:T(8,128)(2,1)} %param.14) | copy-start | bytes 196612
  6.5 167.5 %all-gather.2.cloned.1.call-start = ((), (), s32[]{:S(2)}) async-start(), calls=%async_computation.2 | async-start | bytes 17301504 | tf_op jit(solution)/shard_map/all_gather | solution.py:9
  21.0 471.2 %reduce-scatter.2.cloned.1.call-start = ((), (), s32[]{:S(2)}) async-start(), calls=%async_computation.3 | async-start | bytes 8912896 | tf_op jit(solution)/shard_map/reduce_scatter | solution.py:40
  311.1 181.1 %copy-start.1 = (f32[256]{0:T(256)S(1)}, f32[256]{0:T(256)}, u32[]{:S(2)}) copy-start(f32[256]{0:T(256)} %param.15) | copy-start | bytes 3076
Sparse Core Ops, SparseCore 0:
  21.1 152.8 all-gather.1
  320.5 171.6 reduce-scatter.1
where the time goes:
time: 505 us; the launch traced here: 501 us
  waiting for transfers between devices  323 us (64%)
  local copies, waits for them, and re-layouts  77 us (15%)
  other arithmetic  59.5 us (12%)
  matrix products  14.6 us (3%)
  between operations  14.1 us (3%)
  blocking collectives  13.3 us (3%)
    reduce_scatter x1, waiting for transfers between devices, body(): lax.psum_scatter(terms.astype(jnp.bfloat16), ('col', 'feat'), scatter_dim...  172 us
    all_gather x1, waiting for transfers between devices, body(): sources = lax.all_gather(node_rows, ('row', 'feat'), axis=0, tiled=True)  151 us
    gather x7, local copies, waits for them, and re-layouts, one_turn(): picked = jnp.take(src_blocks, cols_here, axis=0)  45.6 us
    scatter-add x7, other arithmetic, one_turn(): return partial_value.at[rows_here].add(prods)  43.3 us
    while x1, local copies, waits for them, and re-layouts, body(): partial_value = lax.fori_loop(0, turns, one_turn, empty)  22.4 us
    all_to_all x1, blocking collectives, body(): lax.all_to_all(features, 'feat', split_axis=0, concat_axis=1, tiled=True)  13.3 us
    dot_general x7, matrix products, one_turn(): jnp.einsum('tij,tjf->tif', tile_block, picked, preferred_element_type=jnp...  12.2 us
  transfers between devices with their start and end apart: 2, of which 2 were waited for; matrix products, arithmetic and copies ran while one was open for 0% of the time, Pallas kernels for 0%

commit v1 on v0

--- a/solution.py
+++ b/solution.py
@@ -6,7 +6,12 @@
 
 def body(features, tiles, tile_row, tile_col, tile_count, weight, bias):
     node_rows = lax.all_to_all(features, "feat", split_axis=0, concat_axis=1, tiled=True)
-    sources = lax.all_gather(node_rows, ("row", "feat"), axis=0, tiled=True)
+    sources = jnp.concatenate(
+        lax.all_to_all(
+            jnp.stack([node_rows] * lax.axis_size(("row", "feat"))), ("row", "feat"), 0, 0
+        ),
+        axis=0,
+    )
     tile_side = tiles.shape[-1]
     width = sources.shape[1]
     node_dev = features.shape[0] // lax.axis_size("feat")

time: 505 us -> 623 us (1.23)
  waiting for transfers between devices: 323 us -> 450 us
  local copies, waits for them, and re-layouts: 77 us -> 61.1 us
  starting transfers between devices: 0.04 us -> 8.96 us
    all_to_all x0 -> x1, waiting for transfers between devices: none -> 256 us  [body(): lax.all_to_all(jnp.stack([node_rows] * lax.axis_size(('row', 'feat'))), (...]
    all_gather x1 -> x0, waiting for transfers between devices: 151 us -> none  [body(): sources = lax.all_gather(node_rows, ('row', 'feat'), axis=0, tiled=True)]
    while x1 -> x0, local copies, waits for them, and re-layouts: 22.4 us -> none  [body(): partial_value = lax.fori_loop(0, turns, one_turn, empty)]
    reduce_scatter x1, waiting for transfers between devices: 172 us -> 193 us  [body(): lax.psum_scatter(terms.astype(jnp.bfloat16), ('col', 'feat'), scatter_dim...]
    all_to_all x0 -> x1, starting transfers between devices: none -> 8.92 us  [body(): lax.all_to_all(jnp.stack([node_rows] * lax.axis_size(('row', 'feat'))), (...]
    another operation x0 -> x2, local copies, waits for them, and re-layouts: none -> 6.48 us  [body(): jnp.stack([node_rows] * lax.axis_size(('row', 'feat')))]
where the time goes in v1:
time: 623 us; the launch traced here: 620 us
  waiting for transfers between devices  450 us (72%)
  local copies, waits for them, and re-layouts  61.1 us (10%)
  other arithmetic  58.1 us (9%)
  matrix products  14.6 us (2%)
  between operations  14.1 us (2%)
  blocking collectives  13.2 us (2%)
  starting transfers between devices  8.96 us (1%)
    all_to_all x1, waiting for transfers between devices, body(): lax.all_to_all(jnp.stack([node_rows] * lax.axis_size(('row', 'feat'))), (...  256 us
    reduce_scatter x1, waiting for transfers between devices, body(): lax.psum_scatter(terms.astype(jnp.bfloat16), ('col', 'feat'), scatter_dim...  193 us
    gather x7, local copies, waits for them, and re-layouts, one_turn(): picked = jnp.take(src_blocks, cols_here, axis=0)  45.6 us
    scatter-add x7, other arithmetic, one_turn(): return partial_value.at[rows_here].add(prods)  43.3 us
    all_to_all x1, blocking collectives, body(): lax.all_to_all(features, 'feat', split_axis=0, concat_axis=1, tiled=True)  13.2 us
  transfers between devices with their start and end apart: 2, of which 2 were waited for; matrix products, arithmetic and copies ran while one was open for 0% of the time, Pallas kernels for 0%

profile of v1, /device:TPU:1, one launch (start us, length us, event | category | flops | bytes accessed | tf_op | source)
XLA Modules:
  0.0 619.8 jit_solution(4039854854583370831)
XLA Ops:
  6.5 0.0 copy-start
  6.5 1.1 copy.15
  7.6 13.2 %all_to_all.21 = bf16[4,2048,32]{1,2,0:T(8,128)(2,1)S(1)} all-to-all(bf16[4,2048,32]{1,2,0:T(8,128)(2,1)S(1)} %bitcast.17), channel_id=1, replica_groups=mesh['row'=8,'col'=4,'feat'=4] {'feat'}, dimensions={0} | all-to-all | bytes 1048576 | tf_op jit(solution)/shard_map/all_to_all | solution.py:8
  20.9 0.3 copy.12
  21.1 6.2 %stack.5 = bf16[32,2048,128]{2,1,0:T(8,128)(2,1)} broadcast(bf16[2048,128]{1,0:T(8,128)(2,1)S(1)} %copy.12), dimensions={1,2} | broadcast | bytes 17301504 | tf_op jit(solution)/shard_map/stack | solution.py:11
  27.3 0.0 copy-start.1
  27.3 0.0 copy-start.2
  27.3 8.9 %all-to-all-start.1 = ((bf16[32,2048,128]{2,1,0:T(8,128)(2,1)}), bf16[32,2048,128]{2,1,0:T(8,128)(2,1)}, u32[]{:S(2)}, u32[]{:S(2)}) async-start(bf16[32,2048,128]{2,1,0:T(8,128)(2,1)} %stack.5), calls=%async_computation.1 | async-start | bytes 33554432 | tf_op jit(solution)/shard_map/all_to_all | solution.py:10
  36.3 0.0 reduce-scatter.2.cloned.1.call-start
  37.0 0.0 copy-done.1
  37.0 0.0 copy-done.2
  37.1 256.2 %all-to-all-done.1 = bf16[32,2048,128]{2,1,0:T(8,128)(2,1)} async-done(((bf16[32,2048,128]{2,1,0:T(8,128)(2,1)}), bf16[32,2048,128]{2,1,0:T(8,128)(2,1)}, u32[]{:S(2)}, u32[]{:S(2)}) %all-to-all-start.1) | async-done | bytes 16777248 | tf_op jit(solution)/shard_map/all_to_all | solution.py:10
  293.2 7.8 %broadcast_in_dim.28 = f32[256,128,128]{2,1,0:T(8,128)} broadcast(f32[]{:T(128)} %constant.47.clone.1), dimensions={} | broadcast | bytes 16777220 | tf_op jit(solution)/shard_map/broadcast_in_dim | solution.py:39
  301.1 106.8 %while.10 = (s32[]{:T(128)}, f32[256,128,128]{2,1,0:T(8,128)}, s32[]{:T(128)}, s32[384]{0:T(512)S(1)}, s32[]{:T(128)}, /*index=5*/bf16[384,128,128]{2,1,0:T(8,12...) while((s32[]{:T(128)}, f32[256,128,128]{2,1,0:T(8,128)}, ...), condition=%wide.region_2.3_spmd, body=%wide.region_0.2_spmd.sunk | while | flops 135791968 | bytes 12588215 | solution.py:40
  301.1 0.1 compare_select_fusion.4
  301.1 0.7 compare_and_fusion.2
  301.9 6.5 %gather_fusion = bf16[32,128,128]{2,1,0:T(8,128)(2,1)S(1)} fusion(bf16[512,128,128]{2,1,0:T(8,128)(2,1)} %get-tuple-element.155, s32[1024]{0:T(1024)S(1)} %pad_clamp_fusion.2), kind=kCustom, calls=%fused_computation.clone.1 | custom fusion | bytes 2097280 | tf_op jit(solution)/shard_map/while/body/jit(_take)/gather | solution.py:33
  308.4 1.7 convolution_select_fusion.2
  310.1 6.2 %scatter_fusion = f32[256,128,128]{2,1,0:T(8,128)} fusion(f32[256,128,128]{2,1,0:T(8,128)} %get-tuple-element.137, s32[32]{0:T(128)S(1)} %compare_select_fusion.4, f32[32,128,128]{2,1,0:T(8,128)S(1)} %convolution_select_fusion.2), kind=kCustom, calls=%fused_computation.1.clone.1 | custom fusion | flops 524288 | bytes 6291584 | tf_op jit(solution)/shard_map/while/body/scatter-add | solution.py:37
  316.4 0.1 compare_select_fusion.4
  316.5 0.7 compare_and_fusion.2
  317.2 6.5 %gather_fusion = bf16[32,128,128]{2,1,0:T(8,128)(2,1)S(1)} fusion(bf16[512,128,128]{2,1,0:T(8,128)(2,1)} %get-tuple-element.155, s32[1024]{0:T(1024)S(1)} %pad_clamp_fusion.2), kind=kCustom, calls=%fused_computation.clone.1 | custom fusion | bytes 2097280 | tf_op jit(solution)/shard_map/while/body/jit(_take)/gather | solution.py:33
  323.7 1.7 convolution_select_fusion.2
  325.5 6.2 %scatter_fusion = f32[256,128,128]{2,1,0:T(8,128)} fusion(f32[256,128,128]{2,1,0:T(8,128)} %get-tuple-element.137, s32[32]{0:T(128)S(1)} %compare_select_fusion.4, f32[32,128,128]{2,1,0:T(8,128)S(1)} %convolution_select_fusion.2), kind=kCustom, calls=%fused_computation.1.clone.1 | custom fusion | flops 524288 | bytes 6291584 | tf_op jit(solution)/shard_map/while/body/scatter-add | solution.py:37
  331.7 0.1 compare_select_fusion.4
  331.7 0.7 compare_and_fusion.2
  332.5 6.5 %gather_fusion = bf16[32,128,128]{2,1,0:T(8,128)(2,1)S(1)} fusion(bf16[512,128,128]{2,1,0:T(8,128)(2,1)} %get-tuple-element.155, s32[1024]{0:T(1024)S(1)} %pad_clamp_fusion.2), kind=kCustom, calls=%fused_computation.clone.1 | custom fusion | bytes 2097280 | tf_op jit(solution)/shard_map/while/body/jit(_take)/gather | solution.py:33
  339.0 1.7 convolution_select_fusion.2
  340.7 6.1 scatter_fusion
  346.9 0.1 compare_select_fusion.4
  346.9 0.7 compare_and_fusion.2
  347.7 6.5 %gather_fusion = bf16[32,128,128]{2,1,0:T(8,128)(2,1)S(1)} fusion(bf16[512,128,128]{2,1,0:T(8,128)(2,1)} %get-tuple-element.155, s32[1024]{0:T(1024)S(1)} %pad_clamp_fusion.2), kind=kCustom, calls=%fused_computation.clone.1 | custom fusion | bytes 2097280 | tf_op jit(solution)/shard_map/while/body/jit(_take)/gather | solution.py:33
  354.2 1.7 convolution_select_fusion.2
  355.9 6.2 %scatter_fusion = f32[256,128,128]{2,1,0:T(8,128)} fusion(f32[256,128,128]{2,1,0:T(8,128)} %get-tuple-element.137, s32[32]{0:T(128)S(1)} %compare_select_fusion.4, f32[32,128,128]{2,1,0:T(8,128)S(1)} %convolution_select_fusion.2), kind=kCustom, calls=%fused_computation.1.clone.1 | custom fusion | flops 524288 | bytes 6291584 | tf_op jit(solution)/shard_map/while/body/scatter-add | solution.py:37
  362.2 0.1 compare_select_fusion.4
  362.3 0.7 compare_and_fusion.2
  363.0 6.5 %gather_fusion = bf16[32,128,128]{2,1,0:T(8,128)(2,1)S(1)} fusion(bf16[512,128,128]{2,1,0:T(8,128)(2,1)} %get-tuple-element.155, s32[1024]{0:T(1024)S(1)} %pad_clamp_fusion.2), kind=kCustom, calls=%fused_computation.clone.1 | custom fusion | bytes 2097280 | tf_op jit(solution)/shard_map/while/body/jit(_take)/gather | solution.py:33
  369.5 1.7 convolution_select_fusion.2
  371.3 6.2 scatter_fusion
  377.4 0.1 compare_select_fusion.4
  377.5 0.7 compare_and_fusion.2
  378.3 6.5 %gather_fusion = bf16[32,128,128]{2,1,0:T(8,128)(2,1)S(1)} fusion(bf16[512,128,128]{2,1,0:T(8,128)(2,1)} %get-tuple-element.155, s32[1024]{0:T(1024)S(1)} %pad_clamp_fusion.2), kind=kCustom, calls=%fused_computation.clone.1 | custom fusion | bytes 2097280 | tf_op jit(solution)/shard_map/while/body/jit(_take)/gather | solution.py:33
  384.8 1.7 convolution_select_fusion.2
  386.5 6.1 scatter_fusion
  392.7 0.1 compare_select_fusion.4
  392.7 0.7 compare_and_fusion.2
  393.5 6.5 %gather_fusion = bf16[32,128,128]{2,1,0:T(8,128)(2,1)S(1)} fusion(bf16[512,128,128]{2,1,0:T(8,128)(2,1)} %get-tuple-element.155, s32[1024]{0:T(1024)S(1)} %pad_clamp_fusion.2), kind=kCustom, calls=%fused_computation.clone.1 | custom fusion | bytes 2097280 | tf_op jit(solution)/shard_map/while/body/jit(_take)/gather | solution.py:33
  400.0 1.7 convolution_select_fusion.2
  401.7 6.1 scatter_fusion
  407.9 0.0 copy-start.3
  407.9 9.2 %convert_element_type.11 = bf16[256,128,128]{2,1,0:T(8,128)(2,1)} convert(f32[256,128,128]{2,1,0:T(8,128)} %get-tuple-element.48) | non-fusion elementwise | flops 4194304 | bytes 25165824 | tf_op jit(solution)/shard_map/convert_element_type | solution.py:42
  417.1 0.0 reduce-scatter.2.cloned.1.call-update
  417.1 193.4 %reduce-scatter.2.cloned.1.call-done = bf16[2048,128]{1,0:T(8,128)(2,1)} async-done(((bf16[32768,128]{1,0:T(8,128)(2,1)}), bf16[2048,128]{1,0:T(8,128)(2,1)}) %reduce-scatter.2.cloned.1.call-update) | async-done | bytes 524304 | tf_op jit(solution)/shard_map/reduce_scatter | solution.py:45
  610.5 0.0 copy-done
  610.5 0.0 copy-done.3
  610.5 2.4 fusion.7
  (9 shorter events, 0.1 us)
Async XLA Ops:
  6.5 604.0 %copy-start = (bf16[128,256]{1,0:T(8,128)(2,1)S(1)}, bf16[128,256]{1,0:T(8,128)(2,1)}, u32[]{:S(2)}) copy-start(bf16[128,256]{1,0:T(8,128)(2,1)} %param.14) | copy-start | bytes 196612
  27.3 9.6 %copy-start.1 = (s32[1,1,384]{2,1,0:T(1,128)S(1)}, s32[1,1,384]{2,1,0:T(1,128)}, u32[]{:S(2)}) copy-start(s32[1,1,384]{2,1,0:T(1,128)} %param.11) | copy-start | bytes 4612
  27.3 9.7 %copy-start.2 = (s32[1,1,384]{2,1,0:T(1,128)S(1)}, s32[1,1,384]{2,1,0:T(1,128)}, u32[]{:S(2)}) copy-start(s32[1,1,384]{2,1,0:T(1,128)} %param.12) | copy-start | bytes 4612
  27.3 265.9 %all-to-all-start.1 = ((bf16[32,2048,128]{2,1,0:T(8,128)(2,1)}), bf16[32,2048,128]{2,1,0:T(8,128)(2,1)}, u32[]{:S(2)}, u32[]{:S(2)}) async-start(bf16[32,2048,128]{2,1,0:T(8,128)(2,1)} %stack.5), calls=%async_computation.1 | async-start | bytes 33554432 | tf_op jit(solution)/shard_map/all_to_all | solution.py:10
  36.3 574.2 %reduce-scatter.2.cloned.1.call-start = ((), (), s32[]{:S(2)}) async-start(), calls=%async_computation.3 | async-start | bytes 8912896 | tf_op jit(solution)/shard_map/reduce_scatter | solution.py:45
  407.9 202.7 %copy-start.3 = (f32[256]{0:T(256)S(1)}, f32[256]{0:T(256)}, u32[]{:S(2)}) copy-start(f32[256]{0:T(256)} %param.15) | copy-start | bytes 3076
Sparse Core Ops, SparseCore 0:
  417.2 193.2 reduce-scatter.1
